TPU v7x, 512 devices: a whole 4x8x8 slice. The times are simulated.
512 devices in a mesh: pipe: 16 (over z_hi, x), dp: 32 (over y, z_lo, core).
Axes of the slice: x: 4, y: 8, z: 8 (z_hi: 4, z_lo: 2; z = z_hi * 2 + z_lo), core: 2. Of those that a mesh axis runs over, the one named last changes fastest.
Arguments:
- activations: bfloat16 [2, 16, 4096, 6144], P(None, 'pipe', 'dp'), may hold values from -6 to 6
- queries: bfloat16 [2, 16, 4096, 128], P(None, 'pipe', 'dp'), may hold values from -16 to 16
- keys: bfloat16 [2, 16, 4096, 128], P(None, 'pipe', 'dp'), may hold values from -16 to 16
- grad_out: bfloat16 [2, 16, 4096, 128], P(None, 'pipe', 'dp'), may hold values from -0.4375 to 0.4375
- segment_ids: int32 [2, 16, 32, 128], P(None, 'pipe', 'dp'), may hold values from 0 to 3, never falling along the last dimension, each value on 1 to 64 neighbouring positions
Outputs:
- grad_value: bfloat16 [16, 6144, 128], P('pipe', 'dp')
Inputs may be any that keep to these rules, and one draw needn't show every extreme that they name: `segment_ids`: ids restart at 0 in every micro-batch; each document spans 1 to 64 tokens, one exactly that many.
All inputs are finite; a program needn't handle non-finite values.
Results may differ from a plain program's by a relative error of at most 0.0063.
Values sent between devices are 32-bit elements; how exact they have to be, the bound alone decides.
A program may use at most 64 MiB of HBM per device.

v0:
```python
import jax
import jax.numpy as jnp
from jax import lax
from jax.sharding import PartitionSpec as P


def partner(block, axis, distance):
    count = lax.axis_size(axis)
    route = []
    for low in range(count):
        high = low | 1 << distance
        if high != low and high < count:
            route += [(low, high), (high, low)]
    return lax.ppermute(block, axis, route)


def section_partial(acts, query_rows, key_rows, grad_rows, segs):
    length = query_rows.shape[0]
    scores = jnp.dot(query_rows, key_rows.T, preferred_element_type=jnp.float32) / jnp.sqrt(
        jnp.float32(query_rows.shape[1])
    )
    position = jnp.arange(length, dtype=jnp.int32)
    keep = (position[None, :] <= position[:, None]) & (segs[None, :] == segs[:, None])
    masked = jnp.where(keep, scores, jnp.float32(-1e30))
    top = jnp.max(masked, axis=1, keepdims=True)
    weights = jnp.where(keep, jnp.exp(masked - top), jnp.float32(0.0))
    probs = (weights / jnp.sum(weights, axis=1, keepdims=True)).astype(jnp.bfloat16)
    grad_v = jnp.einsum("qk,qd->kd", probs, grad_rows, preferred_element_type=jnp.float32).astype(
        jnp.bfloat16
    )
    return jnp.einsum("td,te->de", acts, grad_v, preferred_element_type=jnp.float32).astype(
        jnp.bfloat16
    )


def body(activations, queries, keys, grad_out, segment_ids):
    partials = []
    for half in range(2):
        partials.append(
            section_partial(
                activations[half, 0],
                queries[half, 0],
                keys[half, 0],
                grad_out[half, 0],
                segment_ids[half, 0, 0],
            )
        )
    lower_part, upper_part = partials
    levels = lax.axis_size("pipe").bit_length() - 1
    stacked = jnp.stack([lower_part.astype(jnp.float32), upper_part.astype(jnp.float32)])
    reduced = lax.psum_scatter(stacked, "dp", scatter_dimension=1, tiled=True)
    lower_sum = reduced[0]
    upper_sum = reduced[1]
    moved = upper_sum
    for level in range(levels):
        moved = partner(moved, "pipe", level)
    total = lower_sum + moved
    return total.astype(jnp.bfloat16)[None]


def solution(mesh):
    return jax.shard_map(
        body,
        mesh=mesh,
        in_specs=(
            P(None, "pipe", "dp", None),
            P(None, "pipe", "dp", None),
            P(None, "pipe", "dp", None),
            P(None, "pipe", "dp", None),
            P(None, "pipe", "dp", None),
        ),
        out_specs=P("pipe", "dp", None),
        check_vma=False,
    )
```

profile of v0, /device:TPU:6, one launch (start us, length us, event | category | flops | bytes accessed | tf_op | source)
XLA Modules:
  0.0 325.4 jit_solution(6235528995120459167)
XLA Ops:
  6.5 0.0 copy-start
  6.5 0.0 all-reduce.3.cloned.1.call-start
  6.5 0.7 slice_bitcast_fusion.1
  7.2 1.0 fusion.53
  8.2 1.0 fusion.54
  9.2 0.1 fusion.11
  9.3 2.2 fusion
  11.5 0.0 copy-done
  11.5 2.2 fusion.1
  13.7 3.1 maximum_convert_fusion
  16.8 10.2 %copy.7 = f32[2,6144,128]{2,0,1:T(2,128)} copy(f32[2,6144,128]{1,2,0:T(8,128)} %maximum_convert_fusion) | data formatting | bytes 12582912 | tf_op jit(solution)/shard_map/stack | solution.py:50
  27.0 0.0 all-reduce.3.cloned.1.call-update
  27.0 1.3 dynamic-slice
  28.9 253.7 %all-reduce.3.cloned.1.call-done = f32[2,6144,128]{2,0,1:T(2,128)} async-done(((f32[2,6144,128]{2,0,1:T(2,128)}), f32[2,6144,128]{2,0,1:T(2,128)}) %all-reduce.3.cloned.1.call-update) | async-done | bytes 6291472
  282.6 1.2 constant_dynamic-slice_fusion.1
  283.8 2.9 collective-permute-start
  286.7 4.1 %collective-permute-done = f32[192,128]{1,0:T(8,128)S(1)} collective-permute-done((f32[192,128]{1,0:T(8,128)S(1)}, f32[192,128]{1,0:T(8,128)S(1)}, u32[]{:S(2)}, u32[]{:S(2)}) %collective-permute-start) | collective-permute-done | bytes 98336 | tf_op jit(solution)/shard_map/ppermute | solution.py:14
  290.9 3.5 %collective-permute-start.1 = (f32[192,128]{1,0:T(8,128)S(1)}, f32[192,128]{1,0:T(8,128)S(1)}, u32[]{:S(2)}, u32[]{:S(2)}) collective-permute-start(f32[192,128]{1,0:T(8,128)S(1)} %collective-permute-done), channel_id=1, source_target_pairs={{0,64},{64,0},{32,96},{96,32},{128,192},{192,128},{160,224},{224,1... | collective-permute-start | bytes 294920 | tf_op jit(solution)/shard_map/ppermute | solution.py:14
  294.4 4.5 %collective-permute-done.1 = f32[192,128]{1,0:T(8,128)S(1)} collective-permute-done((f32[192,128]{1,0:T(8,128)S(1)}, f32[192,128]{1,0:T(8,128)S(1)}, u32[]{:S(2)}, u32[]{:S(2)}) %collective-permute-start.1) | collective-permute-done | bytes 98336 | tf_op jit(solution)/shard_map/ppermute | solution.py:14
  298.9 4.5 %collective-permute-start.2 = (f32[192,128]{1,0:T(8,128)S(1)}, f32[192,128]{1,0:T(8,128)S(1)}, u32[]{:S(2)}, u32[]{:S(2)}) collective-permute-start(f32[192,128]{1,0:T(8,128)S(1)} %collective-permute-done.1), channel_id=1, source_target_pairs={{0,128},{128,0},{32,160},{160,32},{64,192},{192,64},{96,224},{224,... | collective-permute-start | bytes 294920 | tf_op jit(solution)/shard_map/ppermute | solution.py:14
  303.4 2.9 collective-permute-done.2
  306.3 8.9 %collective-permute-start.3 = (f32[192,128]{1,0:T(8,128)S(1)}, f32[192,128]{1,0:T(8,128)S(1)}, u32[]{:S(2)}, u32[]{:S(2)}) collective-permute-start(f32[192,128]{1,0:T(8,128)S(1)} %collective-permute-done.2), channel_id=1, source_target_pairs={{0,256},{256,0},{32,288},{288,32},{64,320},{320,64},{96,352},{352,... | collective-permute-start | bytes 294920 | tf_op jit(solution)/shard_map/ppermute | solution.py:14
  315.2 2.7 collective-permute-done.3
  317.9 0.6 fusion.10
Async XLA Ops:
  6.5 5.0 %copy-start = (bf16[2,1,128,128]{3,2,1,0:T(8,128)(2,1)S(1)}, bf16[2,1,128,128]{3,2,1,0:T(8,128)(2,1)}, u32[]{:S(2)}) copy-start(bf16[2,1,128,128]{3,2,1,0:T(8,128)(2,1)} %param.8) | copy-start | bytes 196612
  6.5 276.1 %all-reduce.3.cloned.1.call-start = ((), (), s32[]{:S(2)}) async-start(), calls=%async_computation | async-start | bytes 12582912
  283.8 7.0 %collective-permute-start = (f32[192,128]{1,0:T(8,128)S(1)}, f32[192,128]{1,0:T(8,128)S(1)}, u32[]{:S(2)}, u32[]{:S(2)}) collective-permute-start(f32[192,128]{1,0:T(8,128)S(1)} %bitcast.54), channel_id=1, source_target_pairs={{0,32},{32,0},{64,96},{96,64},{128,160},{160,128},{192,224},{224,1... | collective-permute-start | bytes 294920 | tf_op jit(solution)/shard_map/ppermute | solution.py:14
  290.9 8.0 %collective-permute-start.1 = (f32[192,128]{1,0:T(8,128)S(1)}, f32[192,128]{1,0:T(8,128)S(1)}, u32[]{:S(2)}, u32[]{:S(2)}) collective-permute-start(f32[192,128]{1,0:T(8,128)S(1)} %collective-permute-done), channel_id=1, source_target_pairs={{0,64},{64,0},{32,96},{96,32},{128,192},{192,128},{160,224},{224,1... | collective-permute-start | bytes 294920 | tf_op jit(solution)/shard_map/ppermute | solution.py:14
  298.9 7.4 %collective-permute-start.2 = (f32[192,128]{1,0:T(8,128)S(1)}, f32[192,128]{1,0:T(8,128)S(1)}, u32[]{:S(2)}, u32[]{:S(2)}) collective-permute-start(f32[192,128]{1,0:T(8,128)S(1)} %collective-permute-done.1), channel_id=1, source_target_pairs={{0,128},{128,0},{32,160},{160,32},{64,192},{192,64},{96,224},{224,... | collective-permute-start | bytes 294920 | tf_op jit(solution)/shard_map/ppermute | solution.py:14
  306.3 11.6 %collective-permute-start.3 = (f32[192,128]{1,0:T(8,128)S(1)}, f32[192,128]{1,0:T(8,128)S(1)}, u32[]{:S(2)}, u32[]{:S(2)}) collective-permute-start(f32[192,128]{1,0:T(8,128)S(1)} %collective-permute-done.2), channel_id=1, source_target_pairs={{0,256},{256,0},{32,288},{288,32},{64,320},{320,64},{96,352},{352,... | collective-permute-start | bytes 294920 | tf_op jit(solution)/shard_map/ppermute | solution.py:14
Sparse Core Ops, SparseCore 0:
  27.1 255.4 all-reduce.2
where the time goes:
time: 326 us; the launch traced here: 325 us
  waiting for transfers between devices  268 us (82%)
  starting transfers between devices  19.9 us (6%)
  between operations  14.1 us (4%)
  local copies, waits for them, and re-layouts  13.3 us (4%)
  matrix products  6.33 us (2%)
  other arithmetic  3.82 us (1%)
    unnamed x2, waiting for transfers between devices  254 us
    ppermute x4, starting transfers between devices, partner(): return lax.ppermute(block, axis, route)  19.9 us
    ppermute x4, waiting for transfers between devices, partner(): return lax.ppermute(block, axis, route)  14.1 us
    another operation x1, local copies, waits for them, and re-layouts, body(): jnp.stack([lower_part.astype(jnp.float32), upper_part.astype(jnp.float32)])  10.2 us
  transfers between devices with their start and end apart: 5, of which 5 were waited for; matrix products, arithmetic and copies ran while one was open for 0% of the time, Pallas kernels for 0%

commit v1 on v0

v1 whole, which is shorter than its diff:
```python
import functools

import jax
import jax.numpy as jnp
from jax import lax
from jax.experimental import pallas as pl
from jax.experimental.pallas import tpu as pltpu
from jax.sharding import PartitionSpec as P

MESH = pl.DeviceIdType.MESH
RING = 8
OFFSETS = (4, 3, -3, 2, -2, 1, -1, 0)
SLOTS = len(OFFSETS)
PLUS = {2: 1, 3: 3, 4: 5}
MINUS = {2: 2, 3: 4, 4: 6}


def transposed_dot(a, b):
    return lax.dot_general(a, b, (((0,), (0,)), ((), ())), preferred_element_type=jnp.float32)


def head_gradient(query_rows, key_rows, grad_rows, segs):
    length, head = query_rows.shape
    scores = lax.dot_general(
        query_rows, key_rows, (((1,), (1,)), ((), ())), preferred_element_type=jnp.float32
    ) / jnp.sqrt(jnp.float32(head))
    across = jnp.broadcast_to(segs.astype(jnp.float32), (length, length))
    down = across.T
    row = lax.broadcasted_iota(jnp.int32, (length, length), 0)
    column = lax.broadcasted_iota(jnp.int32, (length, length), 1)
    keep = (column <= row) & (across == down)
    masked = jnp.where(keep, scores, jnp.float32(-1e30))
    top = jnp.max(masked, axis=1, keepdims=True)
    weights = jnp.where(keep, jnp.exp(masked - top), jnp.float32(0.0))
    probs = (weights / jnp.sum(weights, axis=1, keepdims=True)).astype(jnp.bfloat16)
    return transposed_dot(probs, grad_rows).astype(jnp.bfloat16)


def kernel(
    split, pipes, acts, queries, keys, grads, segs, out,
    q_buf, k_buf, g_buf, s_buf, a_buf, head_grad,
    part, twin, pair, y_first, y_rest, z_first, z_rest, y_tail, z_tail, total,
    load_sem, x_send, x_recv, p_send, p_recv, y_send, y_recv, z_send, z_recv, t_send, t_recv,
):
    pipe, dp = lax.axis_index("pipe"), lax.axis_index("dp")
    y, low, core = dp // 4, (dp // 2) % 2, dp % 2
    rows = out.shape[0]

    def at(pipe_index, y_index, low_index, core_index):
        return {"pipe": pipe_index, "dp": y_index * 4 + low_index * 2 + core_index}

    twin_id = at(pipe, y, low, 1 - core)
    pair_id = at(pipe, y, 1 - low, core)
    plus_id = at(pipe, (y + 1) % RING, low, core)
    minus_id = at(pipe, (y + RING - 1) % RING, low, core)
    mirror_id = at(pipes - 1 - pipe, y, low, core)
    across_id = at(pipes - 1 - pipe, y, 1 - low, core)
    peers = (twin_id, pair_id, plus_id, minus_id, mirror_id, across_id)

    barrier = pltpu.get_barrier_semaphore()
    for peer in peers:
        pl.semaphore_signal(barrier, inc=1, device_id=peer, device_id_type=MESH)

    def load(src, dst, number):
        copy = pltpu.make_async_copy(src, dst, load_sem.at[number])
        copy.start()
        return copy

    small = [
        load(src, dst, number)
        for number, (src, dst) in enumerate(
            ((queries, q_buf), (keys, k_buf), (grads, g_buf), (segs, s_buf))
        )
    ]
    wide = 4 * rows
    large = []
    for slot, offset in enumerate(OFFSETS):
        first = pl.multiple_of(((y + RING + offset) % RING) * wide, 128)
        large.append(load(acts.at[:, :, pl.ds(first, wide)], a_buf.at[slot], 4 + slot))
    for copy in small:
        copy.wait()
    for half in range(2):
        head_grad[half] = head_gradient(q_buf[half], k_buf[half], g_buf[half], s_buf[half])

    started = []

    def send(src, dst, send_sem, recv_sem, peer):
        copy = pltpu.make_async_remote_copy(
            src_ref=src, dst_ref=dst, send_sem=send_sem, recv_sem=recv_sem,
            device_id=peer, device_id_type=MESH,
        )
        copy.start()
        started.append(copy)
        return copy

    def product(slot):
        large[slot].wait()
        for half in range(2):
            block = transposed_dot(a_buf[slot, half], head_grad[half])
            for z in range(2):
                for c in range(2):
                    start = (z * 2 + c) * rows
                    part[slot, c, half, z] = block[start : start + rows]

    exchanges, pairs = [], []

    def trade(slot):
        exchanges.append(
            send(part.at[slot, 1 - core], twin.at[slot], x_send.at[slot], x_recv.at[slot], twin_id)
        )

    def merge(slot):
        exchanges[slot].wait_recv()
        part[slot, core] += twin[slot]
        pairs.append(
            send(
                part.at[slot, core, :, 1 - low, split:], pair.at[slot],
                p_send.at[slot], p_recv.at[slot], pair_id,
            )
        )

    def settle(slot):
        pairs[slot].wait_recv()
        part[slot, core, :, low, split:] += pair[slot]

    ways = (plus_id, minus_id)
    y_copies, z_copies = {}, {}

    def y_start():
        for way in range(2):
            y_copies[1, way] = send(
                part.at[0, core, way, :, :split], y_first.at[way],
                y_send.at[way], y_recv.at[way], ways[way],
            )

    def z_start():
        for way in range(2):
            z_copies[1, way] = send(
                part.at[0, core, way, low, split:], z_first.at[way],
                z_send.at[way], z_recv.at[way], ways[way],
            )

    def y_arrive(step, way, slot):
        y_copies[step, way].wait_recv()
        if step == 1:
            part[slot, core, way, :, :split] += y_first[way]
        else:
            part[slot, core, :, :, :split] += y_rest[way, step - 2]

    def z_arrive(step, way, slot):
        z_copies[step, way].wait_recv()
        if step == 1:
            part[slot, core, way, low, split:] += z_first[way]
        else:
            part[slot, core, :, low, split:] += z_rest[way, step - 2]

    def y_step(step):
        for way, slot in ((0, PLUS[step]), (1, MINUS[step])):
            y_arrive(step - 1, way, slot)
            number = 2 * (step - 1) + way
            y_copies[step, way] = send(
                part.at[slot, core, :, :, :split], y_rest.at[way, step - 2],
                y_send.at[number], y_recv.at[number], ways[way],
            )

    def z_step(step):
        for way, slot in ((0, PLUS[step]), (1, MINUS[step])):
            settle(slot)
            z_arrive(step - 1, way, slot)
            number = 2 * (step - 1) + way
            z_copies[step, way] = send(
                part.at[slot, core, :, low, split:], z_rest.at[way, step - 2],
                z_send.at[number], z_recv.at[number], ways[way],
            )

    last = SLOTS - 1
    for slot in range(SLOTS):
        product(slot)
        if slot == 0:
            pl.semaphore_wait(barrier, len(peers))
        trade(slot)
        if slot >= 2:
            merge(slot - 2)
        if slot == 2:
            y_start()
    merge(last - 1)
    merge(last)
    settle(0)
    z_start()
    for step in (2, 3, 4):
        y_step(step)
        z_step(step)

    tails = []
    for way in range(2):
        y_arrive(4, way, last)
    for number, (half, z, peer) in enumerate(
        ((1, 1 - low, across_id), (1, low, mirror_id), (0, 1 - low, pair_id))
    ):
        tails.append(
            send(
                part.at[last, core, half, z, :split], y_tail.at[number],
                t_send.at[number], t_recv.at[number], peer,
            )
        )
    settle(last)
    for way in range(2):
        z_arrive(4, way, last)
    tails.append(
        send(part.at[last, core, 1, low, split:], z_tail, t_send.at[3], t_recv.at[3], mirror_id)
    )
    for copy in tails:
        copy.wait_recv()
    total[:split] = part[last, core, 0, low, :split] + y_tail[0] + y_tail[1] + y_tail[2]
    total[split:] = part[last, core, 0, low, split:] + z_tail[...]
    out[...] = total[...].astype(out.dtype)
    for copy in started:
        copy.wait_send()


def body(activations, queries, keys, grad_out, segment_ids):
    _, _, length, width = activations.shape
    head = queries.shape[-1]
    count, pipes = lax.axis_size("dp"), lax.axis_size("pipe")
    rows = width // count
    split = rows * 5 // 12 // 8 * 8
    rest = rows - split
    f32, bf16 = jnp.float32, jnp.bfloat16
    dma = lambda *shape: pltpu.SemaphoreType.DMA(shape)
    result = pl.pallas_call(
        functools.partial(kernel, split, pipes),
        out_shape=jax.ShapeDtypeStruct((rows, head), bf16),
        in_specs=[pl.BlockSpec(memory_space=pl.ANY)] * 5,
        out_specs=pl.BlockSpec(memory_space=pltpu.VMEM),
        scratch_shapes=[
            pltpu.VMEM((2, length, head), bf16),
            pltpu.VMEM((2, length, head), bf16),
            pltpu.VMEM((2, length, head), bf16),
            pltpu.VMEM((2, 1, length), jnp.int32),
            pltpu.VMEM((SLOTS, 2, length, 4 * rows), bf16),
            pltpu.VMEM((2, length, head), bf16),
            pltpu.VMEM((SLOTS, 2, 2, 2, rows, head), f32),
            pltpu.VMEM((SLOTS, 2, 2, rows, head), f32),
            pltpu.VMEM((SLOTS, 2, rest, head), f32),
            pltpu.VMEM((2, 2, split, head), f32),
            pltpu.VMEM((2, 3, 2, 2, split, head), f32),
            pltpu.VMEM((2, rest, head), f32),
            pltpu.VMEM((2, 3, 2, rest, head), f32),
            pltpu.VMEM((3, split, head), f32),
            pltpu.VMEM((rest, head), f32),
            pltpu.VMEM((rows, head), f32),
            dma(12), dma(SLOTS), dma(SLOTS), dma(SLOTS), dma(SLOTS),
            dma(8), dma(8), dma(8), dma(8), dma(4), dma(4),
        ],
        compiler_params=pltpu.CompilerParams(
            collective_id=0, has_side_effects=True, vmem_limit_bytes=48 * 2**20
        ),
        name="reduce_value_grad",
    )(
        activations.reshape(2, length, width),
        queries.reshape(2, length, head),
        keys.reshape(2, length, head),
        grad_out.reshape(2, length, head),
        segment_ids.reshape(2, 1, length),
    )
    return result[None]


def solution(mesh):
    return jax.shard_map(
        body,
        mesh=mesh,
        in_specs=(
            P(None, "pipe", "dp", None),
            P(None, "pipe", "dp", None),
            P(None, "pipe", "dp", None),
            P(None, "pipe", "dp", None),
            P(None, "pipe", "dp", None),
        ),
        out_specs=P("pipe", "dp", None),
        check_vma=False,
    )
```

time: 326 us -> 53.1 us (0.16)
  the two profiles are of different devices: /device:TPU:6 before, /device:TPU:64 now
where the time goes in v1:
time: 53.1 us; the launch traced here: 52.8 us
  Pallas kernels  47.1 us (89%)
  local copies, waits for them, and re-layouts  5.71 us (11%)
    pallas_call x1, Pallas kernels, body(): pl.pallas_call(functools.partial(kernel, split, pipes), out_shape=jax.Sha...  47.1 us
    unnamed x11, local copies, waits for them, and re-layouts  5.71 us

profile of v1, /device:TPU:64, one launch (start us, length us, event | category | flops | bytes accessed | tf_op | source)
XLA Modules:
  0.0 52.8 jit_solution(16002190578024566273)
XLA Ops:
  0.0 0.0 copy-start
  0.0 1.9 %copy-done = bf16[2,1,128,6144]{3,2,1,0:T(8,128)(2,1)S(1)} copy-done((bf16[2,1,128,6144]{3,2,1,0:T(8,128)(2,1)S(1)}, bf16[2,1,128,6144]{3,2,1,0:T(8,128)(2,1)}, u32[]{:S(2)}) %copy-start) | copy-done | bytes 3145752
  1.9 0.0 copy-start.1
  1.9 0.8 %copy-done.1 = bf16[2,1,128,128]{3,2,1,0:T(8,128)(2,1)S(1)} copy-done((bf16[2,1,128,128]{3,2,1,0:T(8,128)(2,1)S(1)}, bf16[2,1,128,128]{3,2,1,0:T(8,128)(2,1)}, u32[]{:S(2)}) %copy-start.1) | copy-done | bytes 65560
  2.7 0.0 copy-start.2
  2.7 0.8 %copy-done.2 = bf16[2,1,128,128]{3,2,1,0:T(8,128)(2,1)S(1)} copy-done((bf16[2,1,128,128]{3,2,1,0:T(8,128)(2,1)S(1)}, bf16[2,1,128,128]{3,2,1,0:T(8,128)(2,1)}, u32[]{:S(2)}) %copy-start.2) | copy-done | bytes 65560
  3.6 0.0 copy-start.3
  3.6 0.8 %copy-done.3 = bf16[2,1,128,128]{3,2,1,0:T(8,128)(2,1)S(1)} copy-done((bf16[2,1,128,128]{3,2,1,0:T(8,128)(2,1)S(1)}, bf16[2,1,128,128]{3,2,1,0:T(8,128)(2,1)}, u32[]{:S(2)}) %copy-start.3) | copy-done | bytes 65560
  4.4 0.0 copy-start.4
  4.4 0.7 %copy-done.4 = s32[2,1,1,128]{3,2,1,0:T(1,128)S(1)} copy-done((s32[2,1,1,128]{3,2,1,0:T(1,128)S(1)}, s32[2,1,1,128]{3,2,1,0:T(1,128)}, u32[]{:S(2)}) %copy-start.4) | copy-done | bytes 1048
  5.1 47.1 %reduce_value_grad.1 = bf16[192,128]{1,0:T(8,128)(2,1)S(1)} custom-call(bf16[2,128,6144]{2,1,0:T(8,128)(2,1)S(1)} %bitcast.6, bf16[2,128,128]{2,1,0:T(8,128)(2,1)S(1)} %bitcast.8, bf16[2,128,128]{2,1,0:T(8,128)(2,1)S(1)} %bitcast.9, bf16[2,128,128]{2,1,0:T(8,128)(2,1)S(1)} %bitcast.10, s32[2,1,128]{2,1,0:T(1,128)S(1)} %bitcast.11), custom_call_target="tpu_custom_call" | custom-call | tf_op jit(solution)/shard_map/reduce_value_grad/pallas_call | solution.py:230
  52.2 0.6 %copy.7 = bf16[1,192,128]{2,1,0:T(8,128)(2,1)} copy(bf16[1,192,128]{2,1,0:T(8,128)(2,1)S(1)} %bitcast.7) | data formatting | bytes 98304
Async XLA Ops:
  0.0 1.9 %copy-start = (bf16[2,1,128,6144]{3,2,1,0:T(8,128)(2,1)S(1)}, bf16[2,1,128,6144]{3,2,1,0:T(8,128)(2,1)}, u32[]{:S(2)}) copy-start(bf16[2,1,128,6144]{3,2,1,0:T(8,128)(2,1)} %param.5) | copy-start | bytes 9437188
  1.9 0.8 %copy-start.1 = (bf16[2,1,128,128]{3,2,1,0:T(8,128)(2,1)S(1)}, bf16[2,1,128,128]{3,2,1,0:T(8,128)(2,1)}, u32[]{:S(2)}) copy-start(bf16[2,1,128,128]{3,2,1,0:T(8,128)(2,1)} %param.6) | copy-start | bytes 196612
  2.7 0.8 %copy-start.2 = (bf16[2,1,128,128]{3,2,1,0:T(8,128)(2,1)S(1)}, bf16[2,1,128,128]{3,2,1,0:T(8,128)(2,1)}, u32[]{:S(2)}) copy-start(bf16[2,1,128,128]{3,2,1,0:T(8,128)(2,1)} %param.7) | copy-start | bytes 196612
  3.6 0.8 %copy-start.3 = (bf16[2,1,128,128]{3,2,1,0:T(8,128)(2,1)S(1)}, bf16[2,1,128,128]{3,2,1,0:T(8,128)(2,1)}, u32[]{:S(2)}) copy-start(bf16[2,1,128,128]{3,2,1,0:T(8,128)(2,1)} %param.8) | copy-start | bytes 196612
  4.4 0.7 %copy-start.4 = (s32[2,1,1,128]{3,2,1,0:T(1,128)S(1)}, s32[2,1,1,128]{3,2,1,0:T(1,128)}, u32[]{:S(2)}) copy-start(s32[2,1,1,128]{3,2,1,0:T(1,128)} %param.9) | copy-start | bytes 3076

commit v2 on v1

v2 whole, which is shorter than its diff:
```python
import functools

import jax
import jax.numpy as jnp
from jax import lax
from jax.experimental import pallas as pl
from jax.experimental.pallas import tpu as pltpu
from jax.sharding import PartitionSpec as P

MESH = pl.DeviceIdType.MESH
RING = 8
OFFSETS = (4, 3, -3, 2, -2, 1, -1, 0)
SLOTS = len(OFFSETS)
PLUS = {2: 1, 3: 3, 4: 5}
MINUS = {2: 2, 3: 4, 4: 6}


def transposed_dot(a, b):
    return lax.dot_general(a, b, (((0,), (0,)), ((), ())), preferred_element_type=jnp.float32)


def head_gradient(query_rows, key_rows, grad_rows, segs):
    length, head = query_rows.shape
    scores = lax.dot_general(
        query_rows, key_rows, (((1,), (1,)), ((), ())), preferred_element_type=jnp.float32
    ) / jnp.sqrt(jnp.float32(head))
    across = jnp.broadcast_to(segs.astype(jnp.float32), (length, length))
    down = across.T
    row = lax.broadcasted_iota(jnp.int32, (length, length), 0)
    column = lax.broadcasted_iota(jnp.int32, (length, length), 1)
    keep = (column <= row) & (across == down)
    masked = jnp.where(keep, scores, jnp.float32(-1e30))
    top = jnp.max(masked, axis=1, keepdims=True)
    weights = jnp.where(keep, jnp.exp(masked - top), jnp.float32(0.0))
    probs = (weights / jnp.sum(weights, axis=1, keepdims=True)).astype(jnp.bfloat16)
    return transposed_dot(probs, grad_rows).astype(jnp.bfloat16)


def kernel(
    split, pipes, acts, queries, keys, grads, segs, out,
    q_buf, k_buf, g_buf, s_buf, a_buf, head_grad,
    part, twin, pair, y_first, y_rest, z_first, z_rest, y_tail, z_tail, total,
    load_sem, x_send, x_recv, p_send, p_recv, y_send, y_recv, z_send, z_recv, t_send, t_recv,
    far_sem,
):
    pipe, dp = lax.axis_index("pipe"), lax.axis_index("dp")
    y, low, core = dp // 4, (dp // 2) % 2, dp % 2
    rows = out.shape[0]
    rest = rows - split

    def at(pipe_index, y_index, low_index, core_index):
        return {"pipe": pipe_index, "dp": y_index * 4 + low_index * 2 + core_index}

    twin_id = at(pipe, y, low, 1 - core)
    pair_id = at(pipe, y, 1 - low, core)
    plus_id = at(pipe, (y + 1) % RING, low, core)
    minus_id = at(pipe, (y + RING - 1) % RING, low, core)
    mirror_id = at(pipes - 1 - pipe, y, low, core)
    across_id = at(pipes - 1 - pipe, y, 1 - low, core)
    near = (twin_id, pair_id, plus_id, minus_id)
    distant = (mirror_id, across_id)
    upper = pipe // (pipes // 2)

    barrier = pltpu.get_barrier_semaphore()
    for peer in near:
        pl.semaphore_signal(barrier, inc=1, device_id=peer, device_id_type=MESH)

    @pl.when(upper == 0)
    def _():
        for peer in distant:
            pl.semaphore_signal(barrier, inc=1, device_id=peer, device_id_type=MESH)

    def meet():
        pl.semaphore_wait(barrier, len(near) + len(distant) * upper)

        @pl.when(upper == 1)
        def _():
            for peer in distant:
                pl.semaphore_signal(far_sem, inc=1, device_id=peer, device_id_type=MESH)

    def meet_distant():
        @pl.when(upper == 0)
        def _():
            pl.semaphore_wait(far_sem, len(distant))

    def load(src, dst, number):
        copy = pltpu.make_async_copy(src, dst, load_sem.at[number])
        copy.start()
        return copy

    small = [
        load(src, dst, number)
        for number, (src, dst) in enumerate(
            ((queries, q_buf), (keys, k_buf), (grads, g_buf), (segs, s_buf))
        )
    ]
    wide = 4 * rows
    large = []
    for slot, offset in enumerate(OFFSETS):
        first = pl.multiple_of(((y + RING + offset) % RING) * wide, 128)
        large.append(load(acts.at[:, :, pl.ds(first, wide)], a_buf.at[slot], 4 + slot))
    for copy in small:
        copy.wait()
    for half in (1, 0):
        head_grad[half] = head_gradient(q_buf[half], k_buf[half], g_buf[half], s_buf[half])

    started = []

    def send(src, dst, send_sem, recv_sem, peer):
        copy = pltpu.make_async_remote_copy(
            src_ref=src, dst_ref=dst, send_sem=send_sem, recv_sem=recv_sem,
            device_id=peer, device_id_type=MESH,
        )
        copy.start()
        started.append(copy)
        return copy

    loaded, exchanges, pairs, y_copies, z_copies, tails = set(), {}, {}, {}, {}, {}
    ways = (plus_id, minus_id)
    last = SLOTS - 1

    def product(half, *slots):
        for slot in slots:
            if slot not in loaded:
                loaded.add(slot)
                large[slot].wait()
            block = transposed_dot(a_buf[slot, half], head_grad[half])
            for z in range(2):
                for c in range(2):
                    start = (z * 2 + c) * rows
                    part[slot, c, half, z] = block[start : start + rows]
            if not exchanges:
                meet()
            number = 2 * slot + half
            exchanges[slot, half] = send(
                part.at[slot, 1 - core, half], twin.at[slot, half],
                x_send.at[number], x_recv.at[number], twin_id,
            )

    def merge(half, *slots):
        for slot in slots:
            exchanges[slot, half].wait_recv()
            part[slot, core, half] += twin[slot, half]

    def halve(half, *slots):
        for slot in slots:
            number = 2 * slot + half
            pairs[slot, half] = send(
                part.at[slot, core, half, 1 - low, split:], pair.at[slot, half],
                p_send.at[number], p_recv.at[number], pair_id,
            )

    def settle(half, slot):
        pairs[slot, half].wait_recv()
        part[slot, core, half, low, split:] += pair[slot, half]

    def y_arrive(half, step, way, slot):
        y_copies[half, step, way].wait_recv()
        if step == 1:
            part[slot, core, half, way, :split] += y_first[half, way]
        else:
            part[slot, core, half, :, :split] += y_rest[half, way, step - 2]

    def z_span(way):
        return slice(split + way * (rest // 2), split + (way + 1) * (rest // 2))

    def z_arrive(half, step, way, slot):
        z_copies[half, step, way].wait_recv()
        if step == 1:
            part[slot, core, half, low, z_span(way)] += z_first[half, way]
        else:
            part[slot, core, half, low, split:] += z_rest[half, way, step - 2]

    def y_step(half, step):
        for way in range(2):
            if step == 1:
                src, dst = part.at[0, core, half, way, :split], y_first.at[half, way]
            else:
                slot = (PLUS, MINUS)[way][step]
                y_arrive(half, step - 1, way, slot)
                src, dst = part.at[slot, core, half, :, :split], y_rest.at[half, way, step - 2]
            number = (half * 4 + step - 1) * 2 + way
            y_copies[half, step, way] = send(
                src, dst, y_send.at[number], y_recv.at[number], ways[way]
            )

    def z_step(half, step):
        if step == 1:
            settle(half, 0)
        for way in range(2):
            if step == 1:
                src, dst = part.at[0, core, half, low, z_span(way)], z_first.at[half, way]
            else:
                slot = (PLUS, MINUS)[way][step]
                settle(half, slot)
                z_arrive(half, step - 1, way, slot)
                src, dst = part.at[slot, core, half, low, split:], z_rest.at[half, way, step - 2]
            number = (half * 4 + step - 1) * 2 + way
            z_copies[half, step, way] = send(
                src, dst, z_send.at[number], z_recv.at[number], ways[way]
            )

    def y_end(half):
        for way in range(2):
            y_arrive(half, 4, way, last)
        goals = ((1 - low, across_id), (low, mirror_id)) if half else ((1 - low, pair_id),)
        for number, (z, peer) in enumerate(goals, 0 if half else 2):
            tails[number] = send(
                part.at[last, core, half, z, :split], y_tail.at[number],
                t_send.at[number], t_recv.at[number], peer,
            )

    def z_end(half):
        settle(half, last)
        for way in range(2):
            z_arrive(half, 4, way, last)
        if half:
            tails[3] = send(
                part.at[last, core, half, low, split:], z_tail,
                t_send.at[3], t_recv.at[3], mirror_id,
            )

    product(1, 0)
    product(0, 0)
    product(1, 1, 2)
    merge(1, 0)
    halve(1, 0)
    y_step(1, 1)
    product(0, 1, 2)
    merge(0, 0)
    y_step(0, 1)
    product(1, 3, 4)
    merge(1, 1, 2)
    halve(1, 1, 2)
    product(0, 3, 4)
    merge(0, 1, 2)
    y_step(1, 2)
    product(1, 5, 6, 7)
    merge(1, 3, 4)
    halve(1, 3, 4)
    z_step(1, 1)
    product(0, 5, 6, 7)
    y_step(0, 2)
    merge(1, 5, 6, 7)
    halve(1, 5, 6, 7)
    merge(0, 3, 4, 5, 6, 7)
    halve(0, 0, 1, 2, 3, 4, 5, 6, 7)
    z_step(1, 2)
    y_step(1, 3)
    y_step(0, 3)
    z_step(1, 3)
    y_step(1, 4)
    z_step(1, 4)
    y_step(0, 4)
    z_step(0, 1)
    meet_distant()
    y_end(1)
    z_end(1)
    z_step(0, 2)
    y_end(0)
    z_step(0, 3)
    z_step(0, 4)
    z_end(0)
    for number in sorted(tails):
        tails[number].wait_recv()
    total[:split] = part[last, core, 0, low, :split] + y_tail[0] + y_tail[1] + y_tail[2]
    total[split:] = part[last, core, 0, low, split:] + z_tail[...]
    out[...] = total[...].astype(out.dtype)
    for copy in started:
        copy.wait_send()


def body(activations, queries, keys, grad_out, segment_ids):
    _, _, length, width = activations.shape
    head = queries.shape[-1]
    count, pipes = lax.axis_size("dp"), lax.axis_size("pipe")
    rows = width // count
    split = rows // 2
    rest = rows - split
    f32, bf16 = jnp.float32, jnp.bfloat16
    dma = lambda *shape: pltpu.SemaphoreType.DMA(shape)
    result = pl.pallas_call(
        functools.partial(kernel, split, pipes),
        out_shape=jax.ShapeDtypeStruct((rows, head), bf16),
        in_specs=[pl.BlockSpec(memory_space=pltpu.HBM)] * 5,
        out_specs=pl.BlockSpec(memory_space=pltpu.VMEM),
        scratch_shapes=[
            pltpu.VMEM((2, length, head), bf16),
            pltpu.VMEM((2, length, head), bf16),
            pltpu.VMEM((2, length, head), bf16),
            pltpu.VMEM((2, 1, length), jnp.int32),
            pltpu.VMEM((SLOTS, 2, length, 4 * rows), bf16),
            pltpu.VMEM((2, length, head), bf16),
            pltpu.VMEM((SLOTS, 2, 2, 2, rows, head), f32),
            pltpu.VMEM((SLOTS, 2, 2, rows, head), f32),
            pltpu.VMEM((SLOTS, 2, rest, head), f32),
            pltpu.VMEM((2, 2, split, head), f32),
            pltpu.VMEM((2, 2, 3, 2, split, head), f32),
            pltpu.VMEM((2, 2, rest // 2, head), f32),
            pltpu.VMEM((2, 2, 3, rest, head), f32),
            pltpu.VMEM((3, split, head), f32),
            pltpu.VMEM((rest, head), f32),
            pltpu.VMEM((rows, head), f32),
            dma(4 + SLOTS), dma(2 * SLOTS), dma(2 * SLOTS), dma(2 * SLOTS), dma(2 * SLOTS),
            dma(16), dma(16), dma(16), dma(16), dma(4), dma(4), pltpu.SemaphoreType.REGULAR,
        ],
        compiler_params=pltpu.CompilerParams(
            collective_id=0, has_side_effects=True, vmem_limit_bytes=67_043_328
        ),
        name="reduce_value_grad",
    )(
        activations.reshape(2, length, width),
        queries.reshape(2, length, head),
        keys.reshape(2, length, head),
        grad_out.reshape(2, length, head),
        segment_ids.reshape(2, 1, length),
    )
    return result[None]


def solution(mesh):
    return jax.shard_map(
        body,
        mesh=mesh,
        in_specs=(
            P(None, "pipe", "dp", None),
            P(None, "pipe", "dp", None),
            P(None, "pipe", "dp", None),
            P(None, "pipe", "dp", None),
            P(None, "pipe", "dp", None),
        ),
        out_specs=P("pipe", "dp", None),
        check_vma=False,
    )
```

time: 53.1 us -> 45.1 us (0.85)
  local copies, waits for them, and re-layouts: 5.71 us -> 1.42 us
  Pallas kernels: 47.1 us -> 43.5 us
    unnamed x11 -> x1, local copies, waits for them, and re-layouts: 5.71 us -> 1.42 us
    pallas_call x1, Pallas kernels: 47.1 us -> 43.5 us  [body(): pl.pallas_call(functools.partial(kernel, split, pipes), out_shape=jax.Sha...]
where the time goes in v2:
time: 45.1 us; the launch traced here: 44.9 us
  Pallas kernels  43.5 us (96%)
  local copies, waits for them, and re-layouts  1.42 us (3%)
    pallas_call x1, Pallas kernels, body(): pl.pallas_call(functools.partial(kernel, split, pipes), out_shape=jax.Sha...  43.5 us
    unnamed x1, local copies, waits for them, and re-layouts  1.42 us

profile of v2, /device:TPU:64, one launch (start us, length us, event | category | flops | bytes accessed | tf_op | source)
XLA Modules:
  0.0 44.9 jit_solution(16790939137351798471)
XLA Ops:
  0.0 43.5 %reduce_value_grad.1 = bf16[192,128]{1,0:T(8,128)(2,1)} custom-call(bf16[2,128,6144]{2,1,0:T(8,128)(2,1)} %bitcast.6, bf16[2,128,128]{2,1,0:T(8,128)(2,1)} %bitcast.8, bf16[2,128,128]{2,1,0:T(8,128)(2,1)} %bitcast.9, bf16[2,128,128]{2,1,0:T(8,128)(2,1)} %bitcast.10, s32[2,1,128]{2,1,0:T(1,128)} %bitcast.11), custom_call_target="tpu_custom_call" | custom-call | tf_op jit(solution)/shard_map/reduce_value_grad/pallas_call | solution.py:282
  43.5 1.4 %copy.7 = bf16[1,192,128]{2,1,0:T(8,128)(2,1)} copy(bf16[1,192,128]{2,1,0:T(8,128)(2,1)} %bitcast.7) | data formatting | bytes 98304

commit v3 on v2

v3 whole, which is shorter than its diff:
```python
import functools

import jax
import jax.numpy as jnp
from jax import lax
from jax.experimental import pallas as pl
from jax.experimental.pallas import tpu as pltpu
from jax.sharding import PartitionSpec as P

MESH = pl.DeviceIdType.MESH
RING = 8
OFFSETS = (4, 3, -3, 2, -2, 1, -1, 0)
SLOTS = len(OFFSETS)
GROUPS = (slice(0, 1), slice(1, 3), slice(3, 5), slice(5, 7), slice(7, 8))
UNITS = 14
PLUS = {1: 0, 2: 1, 3: 3, 4: 5}
MINUS = {1: 0, 2: 2, 3: 4, 4: 6}
ORDER = (
    ("P", 1, 0), ("P", 1, 1), ("P", 0, 0), ("M", 1, 0), ("H", 1, 0), ("Y", 1, 1, 0, 0),
    ("Y", 1, 1, 1, 1), ("P", 1, 2), ("P", 0, 4), ("M", 1, 1), ("Y", 1, 2, 0, 1), ("Y", 1, 2, 1, 0),
    ("M", 0, 0), ("H", 1, 1), ("Y", 0, 1, 0, 0), ("P", 1, 3), ("Y", 0, 1, 1, 1), ("P", 0, 2),
    ("P", 0, 1), ("M", 1, 2), ("P", 0, 3), ("Z", 1, 1, 0, 0), ("Z", 1, 1, 1, 1), ("Y", 1, 2, 1, 1),
    ("H", 0, 0), ("Y", 1, 2, 0, 0), ("H", 1, 2), ("M", 1, 3), ("M", 0, 1), ("Y", 1, 3, 1, 0),
    ("Y", 1, 3, 0, 1), ("P", 1, 4), ("Z", 1, 2, 0, 1), ("M", 1, 4), ("Z", 1, 2, 1, 0),
    ("Z", 1, 2, 1, 1), ("Z", 1, 2, 0, 0), ("M", 0, 2), ("H", 1, 3), ("Y", 1, 3, 0, 0),
    ("Y", 1, 3, 1, 1), ("H", 1, 4), ("Y", 1, 4, 1, 0), ("Y", 1, 4, 0, 1), ("M", 0, 3),
    ("Z", 1, 3, 0, 0), ("Z", 1, 3, 0, 1), ("Z", 1, 3, 1, 0), ("H", 0, 2), ("Z", 1, 3, 1, 1),
    ("Y", 1, 4, 0, 0), ("Y", 1, 4, 1, 1), ("Y", 0, 2, 1, 0), ("H", 0, 1), ("Y", 0, 2, 0, 0),
    ("Z", 1, 4, 0, 0), ("Z", 1, 4, 1, 0), ("Z", 1, 4, 0, 1), ("Z", 1, 4, 1, 1), ("Y", 0, 2, 0, 1),
    ("Z", 0, 1, 0, 0), ("Y", 0, 2, 1, 1), ("Z", 0, 1, 1, 1), ("A", 1), ("Y", 0, 3, 1, 0),
    ("Y", 0, 3, 0, 0), ("B", 1), ("M", 0, 4), ("Z", 0, 2, 0, 1), ("Z", 0, 2, 1, 0), ("H", 0, 3),
    ("Y", 0, 3, 0, 1), ("Z", 0, 2, 0, 0), ("Y", 0, 3, 1, 1), ("Z", 0, 2, 1, 1), ("Y", 0, 4, 0, 0),
    ("H", 0, 4), ("Z", 0, 3, 1, 0), ("Y", 0, 4, 1, 0), ("Y", 0, 4, 0, 1), ("Z", 0, 3, 0, 1),
    ("Y", 0, 4, 1, 1), ("Z", 0, 3, 0, 0), ("Z", 0, 3, 1, 1), ("Z", 0, 4, 1, 0), ("Z", 0, 4, 0, 1),
    ("A", 0), ("Z", 0, 4, 0, 0), ("Z", 0, 4, 1, 1), ("B", 0),
)


def transposed_dot(a, b):
    return lax.dot_general(a, b, (((0,), (0,)), ((), ())), preferred_element_type=jnp.float32)


def head_gradient(query_rows, key_rows, grad_rows, segs):
    length, head = query_rows.shape
    scores = lax.dot_general(
        query_rows, key_rows, (((1,), (1,)), ((), ())), preferred_element_type=jnp.float32
    ) / jnp.sqrt(jnp.float32(head))
    across = jnp.broadcast_to(segs.astype(jnp.float32), (length, length))
    down = across.T
    row = lax.broadcasted_iota(jnp.int32, (length, length), 0)
    column = lax.broadcasted_iota(jnp.int32, (length, length), 1)
    keep = (column <= row) & (across == down)
    masked = jnp.where(keep, scores, jnp.float32(-1e30))
    top = jnp.max(masked, axis=1, keepdims=True)
    weights = jnp.where(keep, jnp.exp(masked - top), jnp.float32(0.0))
    probs = (weights / jnp.sum(weights, axis=1, keepdims=True)).astype(jnp.bfloat16)
    return transposed_dot(probs, grad_rows).astype(jnp.bfloat16)


def kernel(
    split, pipes, acts, queries, keys, grads, segs, out,
    q_buf, k_buf, g_buf, s_buf, a_buf, head_grad,
    part, twin, pair, y_buf, z_buf, y_tail, z_tail, total,
    load_sem, x_send, x_recv, p_send, p_recv, y_send, y_recv, z_send, z_recv, t_send, u_send, t_recv,
    far_sem,
):
    pipe, dp = lax.axis_index("pipe"), lax.axis_index("dp")
    y, low, core = dp // 4, (dp // 2) % 2, dp % 2
    rows = out.shape[0]
    rest = rows - split

    def at(pipe_index, y_index, low_index, core_index):
        return {"pipe": pipe_index, "dp": y_index * 4 + low_index * 2 + core_index}

    twin_id = at(pipe, y, low, 1 - core)
    pair_id = at(pipe, y, 1 - low, core)
    plus_id = at(pipe, (y + 1) % RING, low, core)
    minus_id = at(pipe, (y + RING - 1) % RING, low, core)
    mirror_id = at(pipes - 1 - pipe, y, low, core)
    across_id = at(pipes - 1 - pipe, y, 1 - low, core)
    near = (twin_id, pair_id, plus_id, minus_id)
    distant = (mirror_id, across_id)
    upper = pipe // (pipes // 2)

    barrier = pltpu.get_barrier_semaphore()
    for peer in near:
        pl.semaphore_signal(barrier, inc=1, device_id=peer, device_id_type=MESH)

    @pl.when(upper == 0)
    def _():
        for peer in distant:
            pl.semaphore_signal(barrier, inc=1, device_id=peer, device_id_type=MESH)

    def meet():
        pl.semaphore_wait(barrier, len(near) + len(distant) * upper)

        @pl.when(upper == 1)
        def _():
            for peer in distant:
                pl.semaphore_signal(far_sem, inc=1, device_id=peer, device_id_type=MESH)

    def meet_distant():
        @pl.when(upper == 0)
        def _():
            pl.semaphore_wait(far_sem, len(distant))

    def load(src, dst, number):
        copy = pltpu.make_async_copy(src, dst, load_sem.at[number])
        copy.start()
        return copy

    small = [
        load(src, dst, number)
        for number, (src, dst) in enumerate(
            ((queries, q_buf), (keys, k_buf), (grads, g_buf), (segs, s_buf))
        )
    ]
    wide = 4 * rows
    whole = load(acts, a_buf, 4)
    for copy in small:
        copy.wait()

    def prepare(half):
        head_grad[half] = head_gradient(q_buf[half], k_buf[half], g_buf[half], s_buf[half])

    prepare(1)

    def send(src, dst, send_sem, recv_sem, peer):
        copy = pltpu.make_async_remote_copy(
            src_ref=src, dst_ref=dst, send_sem=send_sem, recv_sem=recv_sem,
            device_id=peer, device_id_type=MESH,
        )
        copy.start()
        return copy

    settled = set()
    exchanges, pairs, y_copies, z_copies, tails = {}, {}, {}, {}, {}
    ways = (plus_id, minus_id)
    last = SLOTS - 1

    def product(half, group):
        for slot in range(SLOTS)[GROUPS[group]]:
            if not exchanges:
                whole.wait()
            first = pl.multiple_of(((y + RING + OFFSETS[slot]) % RING) * wide, 128)
            block = transposed_dot(a_buf[half, :, pl.ds(first, wide)], head_grad[half])
            for z in range(2):
                for c in range(2):
                    start = (z * 2 + c) * rows
                    part[slot, c, half, z] = block[start : start + rows]
        if not exchanges:
            meet()
        slots, number = GROUPS[group], 2 * group + half
        exchanges[half, group] = send(
            part.at[slots, 1 - core, half], twin.at[slots, half],
            x_send, x_recv.at[number], twin_id,
        )

        if len(exchanges) == 1:
            prepare(0)

    def merge(half, group):
        exchanges[half, group].wait_recv()
        for slot in range(SLOTS)[GROUPS[group]]:
            part[slot, core, half] += twin[slot, half]

    def halve(half, group):
        slots, number = GROUPS[group], 2 * group + half
        pairs[half, group] = send(
            part.at[slots, core, half, 1 - low, split:], pair.at[slots, half],
            p_send, p_recv.at[number], pair_id,
        )

    def settle(half, group):
        if (half, group) not in settled:
            settled.add((half, group))
            pairs[half, group].wait_recv()
            for slot in range(SLOTS)[GROUPS[group]]:
                part[slot, core, half, low, split:] += pair[slot, half]

    def z_span(piece):
        return slice(split + piece * (rest // 2), split + (piece + 1) * (rest // 2))

    def place(half, step, way, piece):
        return half * UNITS + (way if step == 1 else 4 * step - 6 + 2 * way + piece)

    def arrive(kind, half, step, way, piece, slot):
        copies = y_copies if kind == "Y" else z_copies
        if (half, step, way, piece) in copies:
            copies[half, step, way, piece].wait_recv()
            if kind == "Y":
                part[slot, core, half, piece, :split] += y_buf[place(half, step, way, piece)]
            else:
                part[slot, core, half, low, z_span(piece)] += z_buf[place(half, step, way, piece)]

    def travel(kind, half, step, way, piece):
        slot = (PLUS, MINUS)[way][step]
        if kind == "Z":
            settle(half, step - 1)
        arrive(kind, half, step - 1, way, piece, slot)
        number = place(half, step, way, piece)
        if kind == "Y":
            y_copies[half, step, way, piece] = send(
                part.at[slot, core, half, piece, :split], y_buf.at[number],
                y_send, y_recv.at[number], ways[way],
            )
        else:
            z_copies[half, step, way, piece] = send(
                part.at[slot, core, half, low, z_span(piece)], z_buf.at[number],
                z_send, z_recv.at[number], ways[way],
            )

    def finish_y(half):
        if half:
            meet_distant()
        for way in range(2):
            for piece in range(2):
                arrive("Y", half, 4, way, piece, last)
        goals = ((1 - low, across_id), (low, mirror_id)) if half else ((1 - low, pair_id),)
        for number, (z, peer) in enumerate(goals, 0 if half else 2):
            tails[number] = send(
                part.at[last, core, half, z, :split], y_tail.at[number],
                t_send, t_recv.at[number], peer,
            )

    def finish_z(half):
        settle(half, len(GROUPS) - 1)
        for way in range(2):
            for piece in range(2):
                arrive("Z", half, 4, way, piece, last)
        if half:
            tails[3] = send(
                part.at[last, core, half, low, split:], z_tail,
                u_send, t_recv.at[3], mirror_id,
            )

    actions = {
        "P": product, "M": merge, "H": halve, "A": finish_y, "B": finish_z,
        "Y": functools.partial(travel, "Y"), "Z": functools.partial(travel, "Z"),
    }
    for action, *values in ORDER:
        actions[action](*values)
    for number in sorted(tails):
        tails[number].wait_recv()
    total[:split] = part[last, core, 0, low, :split] + y_tail[0] + y_tail[1] + y_tail[2]
    total[split:] = part[last, core, 0, low, split:] + z_tail[...]
    out[...] = total[...].astype(out.dtype)
    for landed, sem in (
        (twin, x_send), (pair, p_send), (y_buf, y_send), (z_buf, z_send),
        (y_tail, t_send), (z_tail, u_send),
    ):
        pltpu.make_async_remote_copy(
            src_ref=landed, dst_ref=landed, send_sem=sem, recv_sem=t_recv.at[3],
            device_id=twin_id, device_id_type=MESH,
        ).wait_send()


def body(activations, queries, keys, grad_out, segment_ids):
    _, _, length, width = activations.shape
    head = queries.shape[-1]
    count, pipes = lax.axis_size("dp"), lax.axis_size("pipe")
    rows = width // count
    split = rows * 96 // 192
    rest = rows - split
    f32, bf16 = jnp.float32, jnp.bfloat16
    dma = lambda *shape: pltpu.SemaphoreType.DMA(shape)
    result = pl.pallas_call(
        functools.partial(kernel, split, pipes),
        out_shape=jax.ShapeDtypeStruct((rows, head), bf16),
        in_specs=[pl.BlockSpec(memory_space=pltpu.HBM)] * 5,
        out_specs=pl.BlockSpec(memory_space=pltpu.VMEM),
        scratch_shapes=[
            pltpu.VMEM((2, length, head), bf16),
            pltpu.VMEM((2, length, head), bf16),
            pltpu.VMEM((2, length, head), bf16),
            pltpu.VMEM((2, 1, length), jnp.int32),
            pltpu.VMEM((2, length, width), bf16),
            pltpu.VMEM((2, length, head), bf16),
            pltpu.VMEM((SLOTS, 2, 2, 2, rows, head), f32),
            pltpu.VMEM((SLOTS, 2, 2, rows, head), f32),
            pltpu.VMEM((SLOTS, 2, rest, head), f32),
            pltpu.VMEM((2 * UNITS, split, head), f32),
            pltpu.VMEM((2 * UNITS, rest // 2, head), f32),
            pltpu.VMEM((3, split, head), f32),
            pltpu.VMEM((rest, head), f32),
            pltpu.VMEM((rows, head), f32),
            dma(5), dma(), dma(2 * len(GROUPS)), dma(), dma(2 * len(GROUPS)),
            dma(), dma(2 * UNITS), dma(), dma(2 * UNITS), dma(), dma(), dma(4),
            pltpu.SemaphoreType.REGULAR,
        ],
        compiler_params=pltpu.CompilerParams(
            collective_id=0, has_side_effects=True, vmem_limit_bytes=56_500_000
        ),
        name="reduce_value_grad",
    )(
        activations.reshape(2, length, width),
        queries.reshape(2, length, head),
        keys.reshape(2, length, head),
        grad_out.reshape(2, length, head),
        segment_ids.reshape(2, 1, length),
    )
    return result[None]


def solution(mesh):
    return jax.shard_map(
        body,
        mesh=mesh,
        in_specs=(
            P(None, "pipe", "dp", None),
            P(None, "pipe", "dp", None),
            P(None, "pipe", "dp", None),
            P(None, "pipe", "dp", None),
            P(None, "pipe", "dp", None),
        ),
        out_specs=P("pipe", "dp", None),
        check_vma=False,
    )
```

time: 45.1 us -> 40.9 us (0.907)
  the two profiles are of different devices: /device:TPU:64 before, /device:TPU:8 now
where the time goes in v3:
time: 40.9 us; the launch traced here: 40.7 us
  Pallas kernels  39.4 us (96%)
  local copies, waits for them, and re-layouts  1.3 us (3%)
    pallas_call x1, Pallas kernels, body(): pl.pallas_call(functools.partial(kernel, split, pipes), out_shape=jax.Sha...  39.4 us
    unnamed x3, local copies, waits for them, and re-layouts  1.3 us

profile of v3, /device:TPU:8, one launch (start us, length us, event | category | flops | bytes accessed | tf_op | source)
XLA Modules:
  0.0 40.7 jit_solution(3545761917483095645)
XLA Ops:
  0.0 0.0 copy-start
  0.0 0.7 %copy-done = s32[2,1,1,128]{3,2,1,0:T(1,128)S(1)} copy-done((s32[2,1,1,128]{3,2,1,0:T(1,128)S(1)}, s32[2,1,1,128]{3,2,1,0:T(1,128)}, u32[]{:S(2)}) %copy-start) | copy-done | bytes 1048
  0.7 39.4 %reduce_value_grad.1 = bf16[192,128]{1,0:T(8,128)(2,1)S(1)} custom-call(bf16[2,128,6144]{2,1,0:T(8,128)(2,1)} %bitcast.8, bf16[2,128,128]{2,1,0:T(8,128)(2,1)} %bitcast.9, bf16[2,128,128]{2,1,0:T(8,128)(2,1)} %bitcast.10, bf16[2,128,128]{2,1,0:T(8,128)(2,1)} %bitcast.11, s32[2,1,128]{2,1,0:T(1,128)S(1)} %bitcast.7), custom_call_target="tpu_custom_call" | custom-call | tf_op jit(solution)/shard_map/reduce_value_grad/pallas_call | solution.py:267
  40.1 0.6 %copy.7 = bf16[1,192,128]{2,1,0:T(8,128)(2,1)} copy(bf16[1,192,128]{2,1,0:T(8,128)(2,1)S(1)} %bitcast.6) | data formatting | bytes 98304
Async XLA Ops:
  0.0 0.7 %copy-start = (s32[2,1,1,128]{3,2,1,0:T(1,128)S(1)}, s32[2,1,1,128]{3,2,1,0:T(1,128)}, u32[]{:S(2)}) copy-start(s32[2,1,1,128]{3,2,1,0:T(1,128)} %param.9) | copy-start | bytes 3076

commit v4 on v3

--- a/solution.py
+++ b/solution.py
@@ -15,24 +15,43 @@
 UNITS = 14
 PLUS = {1: 0, 2: 1, 3: 3, 4: 5}
 MINUS = {1: 0, 2: 2, 3: 4, 4: 6}
-ORDER = (
-    ("P", 1, 0), ("P", 1, 1), ("P", 0, 0), ("M", 1, 0), ("H", 1, 0), ("Y", 1, 1, 0, 0),
-    ("Y", 1, 1, 1, 1), ("P", 1, 2), ("P", 0, 4), ("M", 1, 1), ("Y", 1, 2, 0, 1), ("Y", 1, 2, 1, 0),
-    ("M", 0, 0), ("H", 1, 1), ("Y", 0, 1, 0, 0), ("P", 1, 3), ("Y", 0, 1, 1, 1), ("P", 0, 2),
-    ("P", 0, 1), ("M", 1, 2), ("P", 0, 3), ("Z", 1, 1, 0, 0), ("Z", 1, 1, 1, 1), ("Y", 1, 2, 1, 1),
-    ("H", 0, 0), ("Y", 1, 2, 0, 0), ("H", 1, 2), ("M", 1, 3), ("M", 0, 1), ("Y", 1, 3, 1, 0),
-    ("Y", 1, 3, 0, 1), ("P", 1, 4), ("Z", 1, 2, 0, 1), ("M", 1, 4), ("Z", 1, 2, 1, 0),
-    ("Z", 1, 2, 1, 1), ("Z", 1, 2, 0, 0), ("M", 0, 2), ("H", 1, 3), ("Y", 1, 3, 0, 0),
-    ("Y", 1, 3, 1, 1), ("H", 1, 4), ("Y", 1, 4, 1, 0), ("Y", 1, 4, 0, 1), ("M", 0, 3),
-    ("Z", 1, 3, 0, 0), ("Z", 1, 3, 0, 1), ("Z", 1, 3, 1, 0), ("H", 0, 2), ("Z", 1, 3, 1, 1),
-    ("Y", 1, 4, 0, 0), ("Y", 1, 4, 1, 1), ("Y", 0, 2, 1, 0), ("H", 0, 1), ("Y", 0, 2, 0, 0),
-    ("Z", 1, 4, 0, 0), ("Z", 1, 4, 1, 0), ("Z", 1, 4, 0, 1), ("Z", 1, 4, 1, 1), ("Y", 0, 2, 0, 1),
-    ("Z", 0, 1, 0, 0), ("Y", 0, 2, 1, 1), ("Z", 0, 1, 1, 1), ("A", 1), ("Y", 0, 3, 1, 0),
-    ("Y", 0, 3, 0, 0), ("B", 1), ("M", 0, 4), ("Z", 0, 2, 0, 1), ("Z", 0, 2, 1, 0), ("H", 0, 3),
-    ("Y", 0, 3, 0, 1), ("Z", 0, 2, 0, 0), ("Y", 0, 3, 1, 1), ("Z", 0, 2, 1, 1), ("Y", 0, 4, 0, 0),
-    ("H", 0, 4), ("Z", 0, 3, 1, 0), ("Y", 0, 4, 1, 0), ("Y", 0, 4, 0, 1), ("Z", 0, 3, 0, 1),
-    ("Y", 0, 4, 1, 1), ("Z", 0, 3, 0, 0), ("Z", 0, 3, 1, 1), ("Z", 0, 4, 1, 0), ("Z", 0, 4, 0, 1),
-    ("A", 0), ("Z", 0, 4, 0, 0), ("Z", 0, 4, 1, 1), ("B", 0),
+LOWER_ORDER = (
+    ("P", 1, 0), ("P", 1, 1), ("M", 1, 0), ("H", 1, 0), ("Y", 1, 1, 1, 1), ("Y", 1, 1, 0, 0),
+    ("P", 0, 0), ("M", 1, 1), ("Y", 1, 2, 1, 0), ("H", 1, 1), ("Y", 1, 2, 0, 1), ("P", 0, 1),
+    ("M", 0, 0), ("Y", 0, 1, 1, 1), ("Y", 0, 1, 0, 0), ("H", 0, 0), ("P", 1, 3), ("P", 1, 2),
+    ("Z", 1, 1, 1, 1), ("Z", 1, 1, 0, 0), ("M", 0, 1), ("Y", 1, 2, 1, 1), ("M", 1, 3),
+    ("Y", 1, 2, 0, 0), ("P", 0, 2), ("M", 1, 2), ("H", 1, 2), ("Y", 1, 3, 1, 0), ("P", 1, 4),
+    ("Y", 1, 3, 0, 1), ("H", 0, 1), ("Y", 0, 2, 1, 0), ("Z", 1, 2, 0, 1), ("Z", 1, 2, 1, 0),
+    ("Z", 1, 2, 1, 1), ("Z", 1, 2, 0, 0), ("Z", 0, 1, 0, 0), ("M", 1, 4), ("Y", 1, 3, 0, 0),
+    ("H", 1, 3), ("Y", 1, 3, 1, 1), ("Y", 0, 2, 0, 1), ("Z", 0, 1, 1, 1), ("M", 0, 2),
+    ("Y", 1, 4, 1, 0), ("Z", 1, 3, 0, 1), ("Z", 1, 3, 1, 0), ("Z", 1, 3, 0, 0), ("Y", 1, 4, 0, 1),
+    ("Z", 1, 3, 1, 1), ("H", 0, 2), ("Y", 1, 4, 0, 0), ("Y", 0, 2, 0, 0), ("H", 1, 4),
+    ("Y", 1, 4, 1, 1), ("P", 0, 4), ("Y", 0, 2, 1, 1), ("Z", 1, 4, 0, 1), ("Z", 1, 4, 0, 0),
+    ("Z", 1, 4, 1, 0), ("Z", 1, 4, 1, 1), ("P", 0, 3), ("Z", 0, 2, 1, 1), ("Z", 0, 2, 0, 1),
+    ("Y", 0, 3, 1, 0), ("Y", 0, 3, 0, 1), ("A", 1), ("Y", 0, 3, 1, 1), ("Y", 0, 3, 0, 0), ("B", 1),
+    ("Z", 0, 2, 0, 0), ("Z", 0, 2, 1, 0), ("M", 0, 4), ("M", 0, 3), ("H", 0, 3), ("Z", 0, 3, 0, 1),
+    ("Z", 0, 3, 1, 1), ("Y", 0, 4, 0, 1), ("Y", 0, 4, 1, 0), ("Y", 0, 4, 0, 0), ("Y", 0, 4, 1, 1),
+    ("Z", 0, 3, 1, 0), ("H", 0, 4), ("Z", 0, 3, 0, 0), ("Z", 0, 4, 0, 1), ("A", 0),
+    ("Z", 0, 4, 1, 1), ("Z", 0, 4, 0, 0), ("Z", 0, 4, 1, 0), ("B", 0),
+)
+UPPER_ORDER = (
+    ("P", 1, 0), ("P", 1, 1), ("M", 1, 0), ("H", 1, 0), ("Y", 1, 1, 1, 1), ("Y", 1, 1, 0, 0),
+    ("P", 1, 4), ("P", 0, 0), ("M", 1, 1), ("Y", 1, 2, 1, 0), ("H", 1, 1), ("Y", 1, 2, 0, 1),
+    ("P", 1, 2), ("M", 0, 0), ("M", 1, 4), ("Y", 0, 1, 1, 1), ("Y", 0, 1, 0, 0), ("P", 0, 2),
+    ("P", 0, 4), ("H", 1, 4), ("M", 1, 2), ("Z", 1, 1, 0, 0), ("Z", 1, 1, 1, 1), ("H", 0, 0),
+    ("Y", 1, 2, 0, 0), ("Y", 1, 2, 1, 1), ("P", 0, 1), ("P", 1, 3), ("Y", 1, 3, 1, 0), ("H", 1, 2),
+    ("Y", 1, 3, 0, 1), ("M", 0, 2), ("Z", 1, 2, 1, 0), ("M", 1, 3), ("M", 0, 4), ("Z", 1, 2, 0, 0),
+    ("Z", 1, 2, 1, 1), ("H", 1, 3), ("Z", 1, 2, 0, 1), ("M", 0, 1), ("P", 0, 3), ("H", 0, 1),
+    ("Y", 1, 3, 0, 0), ("Y", 1, 3, 1, 1), ("H", 0, 2), ("Z", 0, 1, 0, 0), ("Y", 1, 4, 0, 1),
+    ("Y", 1, 4, 1, 0), ("Z", 1, 3, 1, 1), ("Z", 1, 3, 0, 0), ("M", 0, 3), ("Z", 1, 3, 0, 1),
+    ("Z", 1, 3, 1, 0), ("Y", 1, 4, 0, 0), ("Y", 1, 4, 1, 1), ("Y", 0, 2, 0, 0), ("Y", 0, 2, 1, 0),
+    ("Z", 1, 4, 0, 0), ("Z", 1, 4, 1, 1), ("Z", 1, 4, 1, 0), ("Z", 1, 4, 0, 1), ("Y", 0, 2, 0, 1),
+    ("Y", 0, 2, 1, 1), ("Z", 0, 2, 0, 1), ("A", 1), ("Z", 0, 2, 0, 0), ("Z", 0, 2, 1, 0),
+    ("Z", 0, 1, 1, 1), ("Y", 0, 3, 1, 0), ("Y", 0, 3, 0, 0), ("B", 1), ("Y", 0, 3, 1, 1),
+    ("Y", 0, 3, 0, 1), ("Z", 0, 3, 0, 0), ("Z", 0, 3, 0, 1), ("H", 0, 3), ("Z", 0, 2, 1, 1),
+    ("Z", 0, 3, 1, 0), ("Y", 0, 4, 1, 0), ("Y", 0, 4, 0, 0), ("Y", 0, 4, 1, 1), ("Y", 0, 4, 0, 1),
+    ("Z", 0, 3, 1, 1), ("Z", 0, 4, 0, 1), ("Z", 0, 4, 1, 0), ("Z", 0, 4, 0, 0), ("H", 0, 4),
+    ("A", 0), ("Z", 0, 4, 1, 1), ("B", 0),
 )
 
 
@@ -116,7 +135,15 @@
         )
     ]
     wide = 4 * rows
-    whole = load(acts, a_buf, 4)
+    large = []
+    for slot, offset in enumerate(OFFSETS):
+        first = pl.multiple_of(((y + RING + offset) % RING) * wide, 128)
+        large.append(
+            pltpu.make_async_copy(
+                acts.at[:, :, pl.ds(first, wide)], a_buf.at[slot], load_sem.at[4 + slot]
+            )
+        )
+    large[0].start()
     for copy in small:
         copy.wait()
 
@@ -124,6 +151,8 @@
         head_grad[half] = head_gradient(q_buf[half], k_buf[half], g_buf[half], s_buf[half])
 
     prepare(1)
+    for copy in large[1:]:
+        copy.start()
 
     def send(src, dst, send_sem, recv_sem, peer):
         copy = pltpu.make_async_remote_copy(
@@ -133,17 +162,18 @@
         copy.start()
         return copy
 
-    settled = set()
+    loaded, settled = set(), set()
     exchanges, pairs, y_copies, z_copies, tails = {}, {}, {}, {}, {}
+    records = (loaded, settled, exchanges, pairs, y_copies, z_copies, tails)
     ways = (plus_id, minus_id)
     last = SLOTS - 1
 
     def product(half, group):
         for slot in range(SLOTS)[GROUPS[group]]:
-            if not exchanges:
-                whole.wait()
-            first = pl.multiple_of(((y + RING + OFFSETS[slot]) % RING) * wide, 128)
-            block = transposed_dot(a_buf[half, :, pl.ds(first, wide)], head_grad[half])
+            if slot not in loaded:
+                loaded.add(slot)
+                large[slot].wait()
+            block = transposed_dot(a_buf[slot, half], head_grad[half])
             for z in range(2):
                 for c in range(2):
                     start = (z * 2 + c) * rows
@@ -211,7 +241,7 @@
             )
 
     def finish_y(half):
-        if half:
+        if half and not tails:
             meet_distant()
         for way in range(2):
             for piece in range(2):
@@ -229,6 +259,8 @@
             for piece in range(2):
                 arrive("Z", half, 4, way, piece, last)
         if half:
+            if not tails:
+                meet_distant()
             tails[3] = send(
                 part.at[last, core, half, low, split:], z_tail,
                 u_send, t_recv.at[3], mirror_id,
@@ -238,10 +270,18 @@
         "P": product, "M": merge, "H": halve, "A": finish_y, "B": finish_z,
         "Y": functools.partial(travel, "Y"), "Z": functools.partial(travel, "Z"),
     }
-    for action, *values in ORDER:
-        actions[action](*values)
-    for number in sorted(tails):
-        tails[number].wait_recv()
+
+    for side, order in enumerate((LOWER_ORDER, UPPER_ORDER)):
+
+        @pl.when(upper == side)
+        def _():
+            for record in records:
+                record.clear()
+            for action, *values in order:
+                actions[action](*values)
+            for number in sorted(tails):
+                tails[number].wait_recv()
+
     total[:split] = part[last, core, 0, low, :split] + y_tail[0] + y_tail[1] + y_tail[2]
     total[split:] = part[last, core, 0, low, split:] + z_tail[...]
     out[...] = total[...].astype(out.dtype)
@@ -260,7 +300,7 @@
     head = queries.shape[-1]
     count, pipes = lax.axis_size("dp"), lax.axis_size("pipe")
     rows = width // count
-    split = rows * 96 // 192
+    split = rows // 2
     rest = rows - split
     f32, bf16 = jnp.float32, jnp.bfloat16
     dma = lambda *shape: pltpu.SemaphoreType.DMA(shape)
@@ -274,7 +314,7 @@
             pltpu.VMEM((2, length, head), bf16),
             pltpu.VMEM((2, length, head), bf16),
             pltpu.VMEM((2, 1, length), jnp.int32),
-            pltpu.VMEM((2, length, width), bf16),
+            pltpu.VMEM((SLOTS, 2, length, 4 * rows), bf16),
             pltpu.VMEM((2, length, head), bf16),
             pltpu.VMEM((SLOTS, 2, 2, 2, rows, head), f32),
             pltpu.VMEM((SLOTS, 2, 2, rows, head), f32),
@@ -284,20 +324,25 @@
             pltpu.VMEM((3, split, head), f32),
             pltpu.VMEM((rest, head), f32),
             pltpu.VMEM((rows, head), f32),
-            dma(5), dma(), dma(2 * len(GROUPS)), dma(), dma(2 * len(GROUPS)),
+            dma(4 + SLOTS), dma(), dma(2 * len(GROUPS)), dma(), dma(2 * len(GROUPS)),
             dma(), dma(2 * UNITS), dma(), dma(2 * UNITS), dma(), dma(), dma(4),
             pltpu.SemaphoreType.REGULAR,
         ],
         compiler_params=pltpu.CompilerParams(
-            collective_id=0, has_side_effects=True, vmem_limit_bytes=56_500_000
+            collective_id=0, has_side_effects=True, vmem_limit_bytes=48 * 2**20
         ),
         name="reduce_value_grad",
     )(
-        activations.reshape(2, length, width),
-        queries.reshape(2, length, head),
-        keys.reshape(2, length, head),
-        grad_out.reshape(2, length, head),
-        segment_ids.reshape(2, 1, length),
+        *(
+            pltpu.with_memory_space_constraint(operand, pltpu.HBM)
+            for operand in (
+                activations.reshape(2, length, width),
+                queries.reshape(2, length, head),
+                keys.reshape(2, length, head),
+                grad_out.reshape(2, length, head),
+                segment_ids.reshape(2, 1, length),
+            )
+        )
     )
     return result[None]
 

time: 40.9 us -> 39.4 us (0.963)
  the two profiles are of different devices: /device:TPU:8 before, /device:TPU:64 now
where the time goes in v4:
time: 39.4 us; the launch traced here: 39.2 us
  Pallas kernels  38.6 us (98%)
  local copies, waits for them, and re-layouts  0.62 us (2%)
    pallas_call x1, Pallas kernels, body(): pl.pallas_call(functools.partial(kernel, split, pipes), out_shape=jax.Sha...  38.6 us

profile of v4, /device:TPU:64, one launch (start us, length us, event | category | flops | bytes accessed | tf_op | source)
XLA Modules:
  0.0 39.2 jit_solution(11267010160061693329)
XLA Ops:
  0.0 38.6 %reduce_value_grad.1 = bf16[192,128]{1,0:T(8,128)(2,1)S(1)} custom-call(bf16[2,128,6144]{2,1,0:T(8,128)(2,1)} %bitcast.7, bf16[2,128,128]{2,1,0:T(8,128)(2,1)} %bitcast.8, bf16[2,128,128]{2,1,0:T(8,128)(2,1)} %bitcast.9, bf16[2,128,128]{2,1,0:T(8,128)(2,1)} %bitcast.10, s32[2,1,128]{2,1,0:T(1,128)} %bitcast.11), custom_call_target="tpu_custom_call" | custom-call | tf_op jit(solution)/shard_map/reduce_value_grad/pallas_call | solution.py:307
  38.6 0.6 %copy.7 = bf16[1,192,128]{2,1,0:T(8,128)(2,1)} copy(bf16[1,192,128]{2,1,0:T(8,128)(2,1)S(1)} %bitcast.6) | data formatting | bytes 98304

commit v5 on v4

--- a/solution.py
+++ b/solution.py
@@ -300,7 +300,7 @@
     head = queries.shape[-1]
     count, pipes = lax.axis_size("dp"), lax.axis_size("pipe")
     rows = width // count
-    split = rows // 2
+    split = rows * 80 // 192
     rest = rows - split
     f32, bf16 = jnp.float32, jnp.bfloat16
     dma = lambda *shape: pltpu.SemaphoreType.DMA(shape)

time: 39.4 us -> 41.6 us (1.056)
  the two profiles are of different devices: /device:TPU:64 before, /device:TPU:1 now
where the time goes in v5:
time: 41.6 us; the launch traced here: 41.5 us
  Pallas kernels  40.9 us (98%)
  local copies, waits for them, and re-layouts  0.62 us (1%)
    pallas_call x1, Pallas kernels, body(): pl.pallas_call(functools.partial(kernel, split, pipes), out_shape=jax.Sha...  40.9 us

profile of v5, /device:TPU:1, one launch (start us, length us, event | category | flops | bytes accessed | tf_op | source)
XLA Modules:
  0.0 41.5 jit_solution(15579296989392887334)
XLA Ops:
  0.0 40.9 %reduce_value_grad.1 = bf16[192,128]{1,0:T(8,128)(2,1)S(1)} custom-call(bf16[2,128,6144]{2,1,0:T(8,128)(2,1)} %bitcast.7, bf16[2,128,128]{2,1,0:T(8,128)(2,1)} %bitcast.8, bf16[2,128,128]{2,1,0:T(8,128)(2,1)} %bitcast.9, bf16[2,128,128]{2,1,0:T(8,128)(2,1)} %bitcast.10, s32[2,1,128]{2,1,0:T(1,128)} %bitcast.11), custom_call_target="tpu_custom_call" | custom-call | tf_op jit(solution)/shard_map/reduce_value_grad/pallas_call | solution.py:307
  40.9 0.6 %copy.7 = bf16[1,192,128]{2,1,0:T(8,128)(2,1)} copy(bf16[1,192,128]{2,1,0:T(8,128)(2,1)S(1)} %bitcast.6) | data formatting | bytes 98304
